TPU v7x, 128 devices: a whole 4x4x4 slice. The times are simulated.
128 devices in a mesh: expert: 8 (over y_lo, x), tile: 16 (over z, y_hi, core).
Axes of the slice: x: 4, y: 4 (y_hi: 2, y_lo: 2; y = y_hi * 2 + y_lo), z: 4, core: 2. Of those that a mesh axis runs over, the one named last changes fastest.
Arguments:
- activations: bfloat16 [6144, 6144], P(('expert', 'tile')), may hold values from -40 to 40
- expert_ids: int32 [6144, 2], P(('expert', 'tile')), may hold values from 0 to 7, all different within a row; in each aligned block of 48 rows (0 to 47, 48 to 95, ...) at most 24 rows name the same one
Outputs:
- hessian: float32 [8, 6144, 6144], P('expert', 'tile')
- panels: float32 [8, 6144, 1536], P('expert', 'tile')
Inputs may be any that keep to these rules, and one draw needn't show every extreme that they name: `expert_ids`: each row names 2 different experts; within the rows of one device no expert is named more than 24 times, a bound that some block reaches; every expert is named by some row.
All inputs are finite; a program needn't handle non-finite values.
Results may differ from a plain program's by a relative error of at most 0.0003.
Values may be sent and summed in bfloat16 or wider, within the bound.
No kernel may reach another device: no remote copies, remote signals or barrier semaphores. Data moves between devices by JAX's collectives and lax.ppermute only.
A program may use at most 256 MiB of HBM per device.

v0:
```python
import math
import jax
import jax.numpy as jnp
from jax import lax
from jax.sharding import PartitionSpec as P

PANEL = 768
damp_fraction = 0.01


def side_by_side(arrays, axis, split_dim, concat_dim, along):
    widths = [math.prod(a.shape[along:]) for a in arrays]
    both = jnp.concatenate(
        [a.reshape(*a.shape[:along], w) for a, w in zip(arrays, widths)], axis=along
    )
    out = lax.all_to_all(both, axis, split_axis=split_dim, concat_axis=concat_dim, tiled=True)
    blocks = jnp.split(out, [sum(widths[:k]) for k in range(1, len(widths))], axis=along)
    return tuple((b.reshape(*out.shape[:along], *a.shape[along:]) for a, b in zip(arrays, blocks)))


def copy_for_each(x, axis):
    count = lax.axis_size(axis)
    return lax.all_to_all(jnp.broadcast_to(x[None], (count, *x.shape)), axis, 0, 0, tiled=True)


def taken_together(x, axis):
    return copy_for_each(x, axis).sum(axis=0)


def local(activations, expert_ids):
    tile_count = lax.axis_size("tile")
    group_count = lax.axis_size("expert")
    token_count = activations.shape[0]
    feature_width = activations.shape[1]
    capacity = 2 * token_count * expert_ids.shape[1] // group_count
    rows_device = feature_width // tile_count
    tile_index = lax.axis_index("tile")
    expert_iota = jnp.arange(group_count, dtype=jnp.int32)
    global_rows = tile_index * rows_device + jnp.arange(rows_device, dtype=jnp.int32)
    routed = jnp.sum((expert_ids[None][..., None] == expert_iota).astype(jnp.int32), axis=2)
    slot_index = jnp.cumsum(routed, axis=1) - 1
    slot_iota = jnp.arange(capacity, dtype=jnp.int32)
    selector = (routed[..., None] > 0) & (slot_index[..., None] == slot_iota)
    packed = jnp.einsum(
        "nkes,nkd->ensd",
        selector.astype(jnp.bfloat16),
        activations[None],
        preferred_element_type=jnp.float32,
    ).astype(jnp.bfloat16)
    flags = jnp.transpose(jnp.sum(selector.astype(jnp.float32), axis=1), (1, 0, 2)).astype(
        jnp.bfloat16
    )
    send_rows = packed
    send_flags = flags
    send_rows = send_rows.reshape(group_count, capacity, feature_width)
    send_flags = send_flags.reshape(group_count, capacity)
    received_rows, received_flags = side_by_side((send_rows, send_flags), "expert", 0, 0, 2)
    accumulate_received_rows = lax.all_gather(
        received_rows.reshape(group_count * capacity, feature_width), "tile", axis=0, tiled=True
    )
    accumulate_received_flags = lax.all_gather(
        received_flags.reshape(group_count * capacity), "tile", axis=0, tiled=True
    )
    own_columns = lax.dynamic_slice_in_dim(
        accumulate_received_rows, tile_index * rows_device, rows_device, 1
    )
    total = jnp.einsum(
        "tr,tc->rc", own_columns, accumulate_received_rows, preferred_element_type=jnp.float32
    )
    expert_count = jnp.sum(accumulate_received_flags.astype(jnp.float32))
    hessian = total * (2.0 / expert_count)
    diag_mask = global_rows[:, None] == jnp.arange(feature_width, dtype=jnp.int32)[None, :]
    diag_total = taken_together(jnp.sum(jnp.where(diag_mask, hessian, jnp.float32(0.0))), "tile")
    damping = damp_fraction * diag_total / feature_width
    hessian = hessian + jnp.where(diag_mask, damping, jnp.float32(0.0))

    def panel_rows_fetch(members, panel_start):
        placement = (
            panel_start + jnp.arange(PANEL, dtype=jnp.int32)[:, None] == global_rows[None, :]
        ).astype(jnp.float32)
        placed = tuple(
            (
                jnp.dot(placement, member_rows, precision=lax.Precision.HIGHEST)
                for member_rows in members
            )
        )
        return lax.psum(placed, "tile")

    factors = []
    for panel in range(2):
        panel_start = panel * PANEL
        panel_block = hessian[:, panel_start : panel_start + PANEL]
        if factors:
            diagonal_rows, earlier_rows = panel_rows_fetch((panel_block, factors[0]), panel_start)
            panel_block = panel_block - jnp.dot(
                factors[0], earlier_rows.T, precision=lax.Precision.HIGHEST
            )
            diagonal_block = diagonal_rows - jnp.dot(
                earlier_rows, earlier_rows.T, precision=lax.Precision.HIGHEST
            )
        else:
            diagonal_block = panel_rows_fetch((panel_block,), panel_start)[0]
        diagonal_factor = jnp.linalg.cholesky(diagonal_block)
        panel_factor = jax.scipy.linalg.solve_triangular(
            diagonal_factor, panel_block.T, lower=True
        ).T
        column_index = panel_start + jnp.arange(PANEL, dtype=jnp.int32)
        lower_mask = global_rows[:, None] >= column_index[None, :]
        factors.append(jnp.where(lower_mask, panel_factor, jnp.float32(0.0)))
    return (hessian[None], jnp.concatenate(factors, axis=1)[None])


def solution(mesh):
    placed = (P(("expert", "tile"), None), P(("expert", "tile"), None))
    return jax.shard_map(
        local,
        mesh=mesh,
        in_specs=placed,
        out_specs=(P("expert", "tile", None), P("expert", "tile", None)),
        check_vma=False,
    )
```

profile of v0, /device:TPU:0, one launch (start us, length us, event | category | flops | bytes accessed | tf_op | source)
XLA Modules:
  0.0 1108.4 jit_solution(1316372026263907840)
XLA Ops:
  9.4 36.0 %all_to_all.11 = bf16[8,24,6145]{2,1,0:T(8,128)(2,1)S(1)} all-to-all(bf16[8,24,6145]{2,1,0:T(8,128)(2,1)S(1)} %pad_maximum_fusion), channel_id=1, replica_groups=mesh['expert'=8,'tile'=16] {'expert'}, dimensions={0} | all-to-all | bytes 4719360 | tf_op jit(solution)/shard_map/all_to_all | solution.py:16
  49.4 39.8 %all-reduce.1 = bf16[3072]{0:T(1024)(128)(2,1)S(1)} all-reduce(bf16[3072]{0:T(1024)(128)(2,1)S(1)} %dynamic-update-slice.25), channel_id=1, replica_groups=mesh['expert'=8,'tile'=16] {'tile'}, use_global_device_ids=true, to_apply=%add.1 | all-reduce | flops 3072 | bytes 12288
  90.5 162.6 %all-gather.2.cloned.1.call-done = bf16[3072,6144]{1,0:T(8,128)(2,1)} async-done(((bf16[192,6144]{1,0:T(8,128)(2,1)}), bf16[3072,6144]{1,0:T(8,128)(2,1)}) %all-gather.2.cloned.1.call-update) | async-done | bytes 37748752 | tf_op jit(solution)/shard_map/all_gather | solution.py:58
  253.1 24.3 %select_reduce_fusion = (f32[]{:T(128)}, f32[384,6144]{1,0:T(8,128)}) fusion(s32[384]{0:T(512)S(1)} %iota_add_fusion.1, f32[]{:T(128)S(6)} %div.12, bf16[3072,6144]{1,0:T(8,128)(2,1)} %all-gather.2.cloned.1.call-done, s32[]{:T(128)S(6)} %select_n.21), kind=kOutput, calls=%fused_computation.5 | convolution fusion | flops 14504951808 | bytes 49546764 | tf_op jit(solution)/shard_map/tr,tc->rc/dot_general | solution.py:67
  278.5 3.5 all-to-all-start.1
  282.1 7.4 all-to-all-done.1
  290.7 4.9 select_add_fusion
  295.6 3.6 copy-done.2
  299.3 3.6 fusion.8
  302.8 10.6 all-reduce.8.cloned.1.call-start
  313.5 2.4 slice_bitcast_fusion
  315.8 5.0 fusion.5
  320.8 127.3 %all-reduce.6.cloned.1.call-done = f32[768,768]{0,1:T(8,128)} async-done(((f32[768,768]{0,1:T(8,128)}), f32[768,768]{0,1:T(8,128)}) %all-reduce.6.cloned.1.call-update) | async-done | bytes 2359312 | tf_op jit(solution)/shard_map/psum | solution.py:87
  448.1 3.2 copy.49
  454.7 11.7 %cholesky.453 = f32[128,128]{1,0:T(8,128)S(1)} custom-call(f32[128,128]{1,0:T(8,128)S(1)} %cholesky.669), custom_call_target="Cholesky" | custom-call | tf_op jit(solution)/shard_map/jit(cholesky)/cholesky | solution.py:103
  466.6 9.8 custom-call.41
  479.2 11.7 %cholesky.472 = f32[128,128]{1,0:T(8,128)S(1)} custom-call(f32[128,128]{1,0:T(8,128)S(1)} %cholesky.673), custom_call_target="Cholesky" | custom-call | tf_op jit(solution)/shard_map/jit(cholesky)/cholesky | solution.py:103
  491.0 10.2 custom-call.42
  503.1 11.7 %cholesky.493 = f32[128,128]{1,0:T(8,128)S(1)} custom-call(f32[128,128]{1,0:T(8,128)S(1)} %cholesky.678), custom_call_target="Cholesky" | custom-call | tf_op jit(solution)/shard_map/jit(cholesky)/cholesky | solution.py:103
  515.5 9.8 custom-call.43
  527.2 11.9 %cholesky.512 = f32[128,128]{1,0:T(8,128)S(1)} custom-call(f32[128,128]{1,0:T(8,128)S(1)} %cholesky.683), custom_call_target="Cholesky" | custom-call | tf_op jit(solution)/shard_map/jit(cholesky)/cholesky | solution.py:103
  539.8 9.8 custom-call.44
  551.4 11.7 %cholesky.531 = f32[128,128]{1,0:T(8,128)S(1)} custom-call(f32[128,128]{1,0:T(8,128)S(1)} %cholesky.688), custom_call_target="Cholesky" | custom-call | tf_op jit(solution)/shard_map/jit(cholesky)/cholesky | solution.py:103
  563.8 9.8 custom-call.45
  575.1 12.1 %cholesky.548 = f32[128,128]{1,0:T(8,128)S(1)} custom-call(f32[128,128]{1,0:T(8,128)S(1)} %convolution_subtract_fusion.21), custom_call_target="Cholesky" | custom-call | tf_op jit(solution)/shard_map/jit(cholesky)/cholesky | solution.py:103
  593.9 17.5 %while.4 = (s32[]{:T(128)}, f32[768,768]{1,0:T(8,128)}, s32[6,2]{0,1:T(2,128)S(1)}, f32[6,128,128]{2,1,0:T(8,128)S(1)}, s32[]{:T(128)}) while((s32[]{:T(128)}, f32[768,768]{1,0:T(8,128)}, s32[6,2]{0,1:T(2,128)S(1)}, f32[6,128,128]{2,1,0:T(8,128)S(1)}, s32[]{:T(128)}) %tuple.86), condition=%wide.while_cond, body=%wide.while_body.sunk | while | flops 2 | bytes 131181 | solution.py:104
  594.6 2.3 bitcast_dynamic-update-slice_fusion.4
  597.5 2.3 bitcast_dynamic-update-slice_fusion.4
  600.5 2.3 bitcast_dynamic-update-slice_fusion.4
  603.4 2.3 bitcast_dynamic-update-slice_fusion.4
  606.3 2.3 bitcast_dynamic-update-slice_fusion.4
  609.3 2.2 bitcast_dynamic-update-slice_fusion.4
  611.5 59.0 %custom-call.46 = f32[6,128,128]{1,2,0:T(8,128)S(1)} custom-call(f32[6,128,128]{2,1,0:T(8,128)S(1)} %get-tuple-element.18), custom_call_target="InvertDiagBlocksLowerTriangular" | custom-call | tf_op jit(solution)/shard_map/jit(_solve_triangular)/triangular_solve | solution.py:104
  675.8 2.1 convolution_subtract_fusion.10
  678.3 2.4 convolution_subtract_fusion.15
  681.0 2.7 convolution_subtract_fusion.17
  684.3 3.5 fusion.3
  687.8 9.5 fusion.143
  697.3 151.3 %all-reduce.8.cloned.1.call-done = (f32[768,768]{1,0:T(8,128)}, f32[768,768]{0,1:T(8,128)}) async-done(((f32[768,768]{1,0:T(8,128)}, f32[768,768]{0,1:T(8,128)}), (f32[768,768]{1,0:T(8,128)}, f32[768,768]{0,1:T(8,128)})) %all-reduce.8.cloned.1.call-update) | async-done | bytes 4718608 | tf_op jit(solution)/shard_map/psum | solution.py:87
  848.6 9.0 fusion.7
  857.6 6.0 convolution_subtract_fusion
  863.6 2.1 copy.57
  869.1 11.7 %cholesky.563 = f32[128,128]{1,0:T(8,128)S(1)} custom-call(f32[128,128]{1,0:T(8,128)S(1)} %cholesky.692), custom_call_target="Cholesky" | custom-call | tf_op jit(solution)/shard_map/jit(cholesky)/cholesky | solution.py:103
  881.0 9.8 custom-call.47
  893.6 11.7 %cholesky.582 = f32[128,128]{1,0:T(8,128)S(1)} custom-call(f32[128,128]{1,0:T(8,128)S(1)} %cholesky.696), custom_call_target="Cholesky" | custom-call | tf_op jit(solution)/shard_map/jit(cholesky)/cholesky | solution.py:103
  906.7 10.2 custom-call.48
  918.8 11.7 %cholesky.603 = f32[128,128]{1,0:T(8,128)S(1)} custom-call(f32[128,128]{1,0:T(8,128)S(1)} %cholesky.701), custom_call_target="Cholesky" | custom-call | tf_op jit(solution)/shard_map/jit(cholesky)/cholesky | solution.py:103
  931.2 9.8 custom-call.49
  942.9 11.8 %cholesky.622 = f32[128,128]{1,0:T(8,128)S(1)} custom-call(f32[128,128]{1,0:T(8,128)S(1)} %cholesky.706), custom_call_target="Cholesky" | custom-call | tf_op jit(solution)/shard_map/jit(cholesky)/cholesky | solution.py:103
  955.4 9.8 custom-call.50
  967.0 11.7 %cholesky.641 = f32[128,128]{1,0:T(8,128)S(1)} custom-call(f32[128,128]{1,0:T(8,128)S(1)} %cholesky.711), custom_call_target="Cholesky" | custom-call | tf_op jit(solution)/shard_map/jit(cholesky)/cholesky | solution.py:103
  979.4 9.8 custom-call.51
  990.7 11.9 %cholesky.658 = f32[128,128]{1,0:T(8,128)S(1)} custom-call(f32[128,128]{1,0:T(8,128)S(1)} %convolution_subtract_fusion.20), custom_call_target="Cholesky" | custom-call | tf_op jit(solution)/shard_map/jit(cholesky)/cholesky | solution.py:103
  1008.6 17.9 %while.5 = (s32[]{:T(128)}, f32[768,768]{1,0:T(8,128)}, s32[6,2]{0,1:T(2,128)S(1)}, f32[6,128,128]{2,1,0:T(8,128)S(1)}, s32[]{:T(128)}) while((s32[]{:T(128)}, f32[768,768]{1,0:T(8,128)}, s32[6,2]{0,1:T(2,128)S(1)}, f32[6,128,128]{2,1,0:T(8,128)S(1)}, s32[]{:T(128)}) %tuple.99), condition=%wide.while_cond.clone, body=%wide.while_body.clone.sunk | while | flops 2 | bytes 131181 | solution.py:104
  1009.3 2.3 bitcast_dynamic-update-slice_fusion.5
  1012.3 2.3 bitcast_dynamic-update-slice_fusion.5
  1015.3 2.3 bitcast_dynamic-update-slice_fusion.5
  1018.3 2.3 bitcast_dynamic-update-slice_fusion.5
  1021.3 2.3 bitcast_dynamic-update-slice_fusion.5
  1024.3 2.2 bitcast_dynamic-update-slice_fusion.5
  1026.5 59.0 %custom-call.52 = f32[6,128,128]{1,2,0:T(8,128)S(1)} custom-call(f32[6,128,128]{2,1,0:T(8,128)S(1)} %get-tuple-element.19), custom_call_target="InvertDiagBlocksLowerTriangular" | custom-call | tf_op jit(solution)/shard_map/jit(_solve_triangular)/triangular_solve | solution.py:104
  1090.8 2.0 convolution_subtract_fusion.6
  1093.3 2.4 convolution_subtract_fusion.14
  1096.1 2.8 convolution_subtract_fusion.16
  (158 shorter events, 69.0 us)
Async XLA Ops:
  7.2 1.2 copy-start
  7.2 245.9 %all-gather.2.cloned.1.call-start = ((), (), s32[]{:S(2)}) async-start(), calls=%async_computation.2 | async-start | bytes 40108032 | tf_op jit(solution)/shard_map/all_gather | solution.py:58
  47.1 0.7 copy-start.12
  278.5 10.9 all-to-all-start.1
  282.0 166.1 %all-reduce.6.cloned.1.call-start = ((), (), s32[]{:S(2)}) async-start(), calls=%async_computation.3 | async-start | bytes 4718592 | tf_op jit(solution)/shard_map/psum | solution.py:87
  295.6 3.6 copy-start.2
  302.8 545.7 %all-reduce.8.cloned.1.call-start = ((), (), s32[]{:S(2)}) async-start(), calls=%async_computation.4 | async-start | bytes 9437184 | tf_op jit(solution)/shard_map/psum | solution.py:87
  448.1 3.2 copy-start.6
  453.3 1.4 copy-start.8
  593.9 79.7 %copy-start.9 = (f32[768,384]{0,1:T(8,128)S(1)}, f32[768,384]{0,1:T(8,128)}, u32[]{:S(2)}) copy-start(f32[768,384]{0,1:T(8,128)} %slice_bitcast_fusion) | copy-start | bytes 3538948
  684.2 164.3 %copy-start.4 = (f32[384,768]{0,1:T(8,128)}, f32[384,768]{0,1:T(8,128)S(1)}, u32[]{:S(2)}) copy-start(f32[384,768]{0,1:T(8,128)S(1)} %bitcast_select_fusion.1) | copy-start | bytes 3538948
  848.6 9.0 copy-start.3
  848.6 9.0 copy-start.11
  867.7 1.4 copy-start.7
  1008.6 80.1 %copy-start.10 = (f32[768,384]{0,1:T(8,128)S(1)}, f32[768,384]{0,1:T(8,128)}, u32[]{:S(2)}) copy-start(f32[768,384]{0,1:T(8,128)} %fusion.7) | copy-start | bytes 3538948
  1096.1 3.4 copy-start.5
  1099.5 2.1 copy-start.1
Sparse Core Ops, SparseCore 0:
  47.2 205.8 all-gather.1
  303.0 145.0 all-reduce.5
  687.9 160.6 all-reduce.7
where the time goes:
time: 1120 us; the launch traced here: 1110 us
  waiting for transfers between devices  449 us (40%)
  other arithmetic  390 us (35%)
  matrix products  98.9 us (9%)
  blocking collectives  75.8 us (7%)
  local copies, waits for them, and re-layouts  56.5 us (5%)
  between operations  24.1 us (2%)
  starting transfers between devices  14.1 us (1%)
    psum x2, waiting for transfers between devices, panel_rows_fetch(): return lax.psum(placed, 'tile')  279 us
    another operation x45, other arithmetic, local(): diagonal_factor = jnp.linalg.cholesky(diagonal_block)  248 us
    all_gather x1, waiting for transfers between devices, local(): lax.all_gather(received_rows.reshape(group_count * capacity, feature_widt...  163 us
    another operation x5, other arithmetic, local(): jax.scipy.linalg.solve_triangular(diagonal_factor, panel_block.T, lower=T...  121 us
    unnamed x1, blocking collectives  39.8 us
    all_to_all x1, blocking collectives, side_by_side(): lax.all_to_all(both, axis, split_axis=split_dim, concat_axis=concat_dim,...  36 us
    another operation x39, local copies, waits for them, and re-layouts, local(): jax.scipy.linalg.solve_triangular(diagonal_factor, panel_block.T, lower=T...  35.3 us
    another operation x22, matrix products, local(): jax.scipy.linalg.solve_triangular(diagonal_factor, panel_block.T, lower=T...  27.3 us
  transfers between devices with their start and end apart: 4, of which 4 were waited for; matrix products, arithmetic and copies ran while one was open for 2% of the time, Pallas kernels for 0%

commit v1 on v0

--- a/solution.py
+++ b/solution.py
@@ -1,3 +1,4 @@
+import functools
 import math
 import jax
 import jax.numpy as jnp
@@ -6,6 +7,22 @@
 
 PANEL = 768
 damp_fraction = 0.01
+
+
+def launch_the_forms(shard_in, chip_axis):
+    step_out = jnp.concatenate(
+        jax.lax.all_to_all(
+            jnp.stack(jax.lax.axis_size(chip_axis) * [shard_in], axis=0),
+            axis_name=chip_axis,
+            split_axis=0,
+            concat_axis=0,
+        ),
+        0,
+    )
+    return step_out
+
+
+view_pipes = functools.partial(launch_the_forms, chip_axis="tile")
 
 
 def side_by_side(arrays, axis, split_dim, concat_dim, along):
@@ -55,8 +72,8 @@
     send_rows = send_rows.reshape(group_count, capacity, feature_width)
     send_flags = send_flags.reshape(group_count, capacity)
     received_rows, received_flags = side_by_side((send_rows, send_flags), "expert", 0, 0, 2)
-    accumulate_received_rows = lax.all_gather(
-        received_rows.reshape(group_count * capacity, feature_width), "tile", axis=0, tiled=True
+    accumulate_received_rows = view_pipes(
+        received_rows.reshape(group_count * capacity, feature_width)
     )
     accumulate_received_flags = lax.all_gather(
         received_flags.reshape(group_count * capacity), "tile", axis=0, tiled=True

time: 1120 us -> 1370 us (1.22)
  blocking collectives: 75.8 us -> 472 us
  waiting for transfers between devices: 449 us -> 284 us
    unnamed x1, blocking collectives: 39.8 us -> 436 us
    all_gather x1 -> x0, waiting for transfers between devices: 163 us -> none  [local(): lax.all_gather(received_rows.reshape(group_count * capacity, feature_widt...]
  transfers between devices with their start and end apart: 4 -> 4, of which waited for: 4 -> 3; matrix products, arithmetic and copies ran while one was open for 2% -> 1% of each run, Pallas kernels for 0% -> 0%
where the time goes in v1:
time: 1370 us; the launch traced here: 1360 us
  blocking collectives  472 us (34%)
  other arithmetic  390 us (28%)
  waiting for transfers between devices  284 us (21%)
  matrix products  99 us (7%)
  local copies, waits for them, and re-layouts  67.1 us (5%)
  between operations  24.6 us (2%)
  starting transfers between devices  22 us (2%)
    unnamed x1, blocking collectives  436 us
    psum x2, waiting for transfers between devices, panel_rows_fetch(): return lax.psum(placed, 'tile')  277 us
    another operation x45, other arithmetic, local(): diagonal_factor = jnp.linalg.cholesky(diagonal_block)  248 us
    another operation x5, other arithmetic, local(): jax.scipy.linalg.solve_triangular(diagonal_factor, panel_block.T, lower=T...  121 us
    all_to_all x1, blocking collectives, side_by_side(): lax.all_to_all(both, axis, split_axis=split_dim, concat_axis=concat_dim,...  36 us
    another operation x39, local copies, waits for them, and re-layouts, local(): jax.scipy.linalg.solve_triangular(diagonal_factor, panel_block.T, lower=T...  35.3 us
  transfers between devices with their start and end apart: 4, of which 3 were waited for; matrix products, arithmetic and copies ran while one was open for 1% of the time, Pallas kernels for 0%

profile of v1, /device:TPU:0, one launch (start us, length us, event | category | flops | bytes accessed | tf_op | source)
XLA Modules:
  0.0 1359.8 jit_solution(16586376367905515183)
XLA Ops:
  9.4 36.0 %all_to_all.16 = bf16[8,24,6145]{2,1,0:T(8,128)(2,1)S(1)} all-to-all(bf16[8,24,6145]{2,1,0:T(8,128)(2,1)S(1)} %pad_maximum_fusion), channel_id=1, replica_groups=mesh['expert'=8,'tile'=16] {'expert'}, dimensions={0} | all-to-all | bytes 4719360 | tf_op jit(solution)/shard_map/all_to_all | solution.py:33
  45.6 12.5 stack.3
  58.1 7.9 all-to-all-start.1
  67.8 436.4 %all-reduce.1 = bf16[3072]{0:T(1024)(128)(2,1)S(1)} all-reduce(bf16[3072]{0:T(1024)(128)(2,1)S(1)} %dynamic-update-slice.25), channel_id=1, replica_groups=mesh['expert'=8,'tile'=16] {'tile'}, use_global_device_ids=true, to_apply=%add.1 | all-reduce | flops 3072 | bytes 12288
  505.5 24.3 %select_reduce_fusion = (f32[]{:T(128)}, f32[384,6144]{1,0:T(8,128)}) fusion(s32[384]{0:T(512)S(1)} %iota_add_fusion.1, f32[]{:T(128)S(6)} %div.12, bf16[3072,6144]{1,0:T(8,128)(2,1)} %bitcast.3, s32[]{:T(128)S(6)} %select_n.21), kind=kOutput, calls=%fused_computation.5 | convolution fusion | flops 14504951808 | bytes 49546764 | tf_op jit(solution)/shard_map/tr,tc->rc/dot_general | solution.py:84
  531.0 3.5 all-to-all-start.2
  534.5 7.4 all-to-all-done.2
  543.2 4.9 select_add_fusion
  548.1 3.6 copy-done.2
  551.7 3.6 fusion.8
  555.3 10.6 all-reduce.8.cloned.1.call-start
  566.0 2.4 slice_bitcast_fusion
  568.3 5.0 fusion.5
  573.3 125.7 %all-reduce.6.cloned.1.call-done = f32[768,768]{0,1:T(8,128)} async-done(((f32[768,768]{0,1:T(8,128)}), f32[768,768]{0,1:T(8,128)}) %all-reduce.6.cloned.1.call-update) | async-done | bytes 2359312 | tf_op jit(solution)/shard_map/psum | solution.py:104
  699.0 3.2 copy.49
  705.6 11.7 cholesky.453
  717.5 9.8 custom-call.41
  730.1 11.7 cholesky.472
  741.8 10.2 custom-call.42
  754.0 11.7 cholesky.493
  766.4 9.8 custom-call.43
  778.1 11.9 cholesky.512
  790.7 9.8 custom-call.44
  802.3 11.7 cholesky.531
  814.7 9.8 custom-call.45
  826.0 12.1 cholesky.548
  844.8 17.5 %while.4 = (s32[]{:T(128)}, f32[768,768]{1,0:T(8,128)}, s32[6,2]{0,1:T(2,128)S(1)}, f32[6,128,128]{2,1,0:T(8,128)S(1)}, s32[]{:T(128)}) while((s32[]{:T(128)}, f32[768,768]{1,0:T(8,128)}, s32[6,2]{0,1:T(2,128)S(1)}, f32[6,128,128]{2,1,0:T(8,128)S(1)}, s32[]{:T(128)}) %tuple.86), condition=%wide.while_cond, body=%wide.while_body.sunk | while | flops 2 | bytes 131181 | solution.py:121
  845.5 2.3 bitcast_dynamic-update-slice_fusion.4
  848.4 2.3 bitcast_dynamic-update-slice_fusion.4
  851.4 2.3 bitcast_dynamic-update-slice_fusion.4
  854.3 2.3 bitcast_dynamic-update-slice_fusion.4
  857.2 2.3 bitcast_dynamic-update-slice_fusion.4
  860.2 2.2 bitcast_dynamic-update-slice_fusion.4
  862.4 59.0 %custom-call.46 = f32[6,128,128]{1,2,0:T(8,128)S(1)} custom-call(f32[6,128,128]{2,1,0:T(8,128)S(1)} %get-tuple-element.18), custom_call_target="InvertDiagBlocksLowerTriangular" | custom-call | tf_op jit(solution)/shard_map/jit(_solve_triangular)/triangular_solve | solution.py:121
  926.7 2.1 convolution_subtract_fusion.10
  929.1 2.4 convolution_subtract_fusion.15
  931.9 2.7 convolution_subtract_fusion.17
  935.2 3.5 fusion.3
  938.7 9.5 fusion.143
  948.2 151.3 %all-reduce.8.cloned.1.call-done = (f32[768,768]{1,0:T(8,128)}, f32[768,768]{0,1:T(8,128)}) async-done(((f32[768,768]{1,0:T(8,128)}, f32[768,768]{0,1:T(8,128)}), (f32[768,768]{1,0:T(8,128)}, f32[768,768]{0,1:T(8,128)})) %all-reduce.8.cloned.1.call-update) | async-done | bytes 4718608 | tf_op jit(solution)/shard_map/psum | solution.py:104
  1099.5 9.0 fusion.7
  1108.5 6.0 convolution_subtract_fusion
  1114.5 2.1 copy.57
  1120.0 11.7 cholesky.563
  1131.9 9.8 custom-call.47
  1144.6 11.7 cholesky.582
  1157.7 10.2 custom-call.48
  1169.8 11.7 cholesky.603
  1182.1 9.8 custom-call.49
  1193.8 11.8 cholesky.622
  1206.4 9.8 custom-call.50
  1218.0 11.7 cholesky.641
  1230.3 9.8 custom-call.51
  1241.7 11.9 cholesky.658
  1259.5 17.9 %while.5 = (s32[]{:T(128)}, f32[768,768]{1,0:T(8,128)}, s32[6,2]{0,1:T(2,128)S(1)}, f32[6,128,128]{2,1,0:T(8,128)S(1)}, s32[]{:T(128)}) while((s32[]{:T(128)}, f32[768,768]{1,0:T(8,128)}, s32[6,2]{0,1:T(2,128)S(1)}, f32[6,128,128]{2,1,0:T(8,128)S(1)}, s32[]{:T(128)}) %tuple.97), condition=%wide.while_cond.clone, body=%wide.while_body.clone.sunk | while | flops 2 | bytes 131181 | solution.py:121
  1260.2 2.3 bitcast_dynamic-update-slice_fusion.5
  1263.2 2.3 bitcast_dynamic-update-slice_fusion.5
  1266.2 2.3 bitcast_dynamic-update-slice_fusion.5
  1269.2 2.3 bitcast_dynamic-update-slice_fusion.5
  1272.2 2.3 bitcast_dynamic-update-slice_fusion.5
  1275.2 2.2 bitcast_dynamic-update-slice_fusion.5
  1277.5 59.0 %custom-call.52 = f32[6,128,128]{1,2,0:T(8,128)S(1)} custom-call(f32[6,128,128]{2,1,0:T(8,128)S(1)} %get-tuple-element.19), custom_call_target="InvertDiagBlocksLowerTriangular" | custom-call | tf_op jit(solution)/shard_map/jit(_solve_triangular)/triangular_solve | solution.py:121
  1344.2 2.4 convolution_subtract_fusion.14
  1347.0 2.8 convolution_subtract_fusion.16
  (158 shorter events, 69.0 us)
Async XLA Ops:
  7.2 1.1 copy-start
  58.1 8.0 copy-start.12
  58.1 447.4 %all-to-all-start.1 = ((bf16[16,192,6144]{2,1,0:T(8,128)(2,1)}), bf16[16,192,6144]{2,1,0:T(8,128)(2,1)}, u32[]{:S(2)}, u32[]{:S(2)}) async-start(bf16[16,192,6144]{2,1,0:T(8,128)(2,1)} %stack.3), calls=%async_computation.1 | async-start | bytes 75497472 | tf_op jit(solution)/shard_map/all_to_all | solution.py:14
  531.0 10.9 all-to-all-start.2
  534.5 164.5 %all-reduce.6.cloned.1.call-start = ((), (), s32[]{:S(2)}) async-start(), calls=%async_computation.3 | async-start | bytes 4718592 | tf_op jit(solution)/shard_map/psum | solution.py:104
  548.1 3.6 copy-start.2
  555.3 544.2 %all-reduce.8.cloned.1.call-start = ((), (), s32[]{:S(2)}) async-start(), calls=%async_computation.4 | async-start | bytes 9437184 | tf_op jit(solution)/shard_map/psum | solution.py:104
  699.0 3.2 copy-start.6
  704.1 1.4 copy-start.8
  844.8 79.7 %copy-start.9 = (f32[768,384]{0,1:T(8,128)S(1)}, f32[768,384]{0,1:T(8,128)}, u32[]{:S(2)}) copy-start(f32[768,384]{0,1:T(8,128)} %slice_bitcast_fusion) | copy-start | bytes 3538948
  935.1 164.4 %copy-start.4 = (f32[384,768]{0,1:T(8,128)}, f32[384,768]{0,1:T(8,128)S(1)}, u32[]{:S(2)}) copy-start(f32[384,768]{0,1:T(8,128)S(1)} %bitcast_select_fusion.1) | copy-start | bytes 3538948
  1099.5 9.0 copy-start.3
  1099.5 9.0 copy-start.11
  1118.6 1.4 copy-start.7
  1259.5 80.1 %copy-start.10 = (f32[768,384]{0,1:T(8,128)S(1)}, f32[768,384]{0,1:T(8,128)}, u32[]{:S(2)}) copy-start(f32[768,384]{0,1:T(8,128)} %fusion.7) | copy-start | bytes 3538948
  1347.0 3.4 copy-start.5
  1350.4 2.1 copy-start.1
Sparse Core Ops, SparseCore 0:
  555.5 143.4 all-reduce.5
  938.8 160.6 all-reduce.7
